TPU v7x, 32 devices: a whole 2x2x4 slice. The times are simulated.
32 devices in a mesh: wave: 4 (over y, x), row: 8 (over z, core).
Axes of the slice: x: 2, y: 2, z: 4, core: 2. Of those that a mesh axis runs over, the one named last changes fastest.
Arguments:
- plane_waves: float32 [2, 4, 2048, 2048], P(None, 'wave', 'row'), may hold values from -6 to 6
- transmission: float32 [1, 2, 2048, 2048], P(None, None, 'row')
- wave_index: int32 [4, 2], P('wave'), may hold values from -32 to 31
- wave_weight: float32 [4], P('wave'), may hold values from 0.3 to 3
- wave_phase: float32 [4], P('wave'), may hold values from -3.140625 to 3.140625
- probe_pos: int32 [64, 2], replicated, may hold values from 0 to 2047, as said below
Outputs:
- diffraction: float32 [64, 128, 128], P('row', 'wave')
Inputs may be any that keep to these rules, and one draw needn't show every extreme that they name: `probe_pos`: the probes numbered j * 8 to (j + 1) * 8 - 1 have their grid row (first entry) in j * 256 to (j + 1) * 256 - 1; the second entry is the grid column.
All inputs are finite; a program needn't handle non-finite values.
Results may differ from a plain program's by a relative error of at most 0.0003.
Values sent between devices are 32-bit elements; how exact they have to be, the bound alone decides.
No kernel may reach another device: no remote copies, remote signals or barrier semaphores. Data moves between devices by JAX's collectives and lax.ppermute only.
A program may use at most 128 MiB of HBM per device.

v0:
```python
import math
import jax
import jax.numpy as jnp
from jax import lax
from jax.sharding import PartitionSpec as P

GRID = 2048
RADIX = 64
FACTOR = 16
WINDOW = 128
HALF = 64
FRESNEL = 0.1
EXACT_PRECISION = lax.Precision.HIGHEST


def padded(block, sides, width):
    for axis, dim in sides:
        count = lax.axis_size(axis)
        forward = [(i, i + 1) for i in range(count - 1)]
        forward.append((count - 1, 0))
        backward = [(target, source) for source, target in forward]
        low = lax.ppermute(
            lax.slice_in_dim(block, block.shape[dim] - width, None, axis=dim), axis, forward
        )
        high = lax.ppermute(lax.slice_in_dim(block, 0, width, axis=dim), axis, backward)
        block = jnp.concatenate([low, block, high], axis=dim)
    return block


def tables(length, direction_sign):
    indices = jnp.arange(length, dtype=jnp.int32)
    product = indices[:, None] * indices[None, :] % length
    angles = product.astype(jnp.float32) * (2.0 * math.pi / length)
    return (jnp.cos(angles), direction_sign * jnp.sin(angles))


def twiddle(outer_len, direction_sign):
    outer_idx = jnp.arange(outer_len, dtype=jnp.int32)
    inner_idx = jnp.arange(RADIX, dtype=jnp.int32)
    product = outer_idx[:, None] * inner_idx[None, :] % GRID
    angles = product.astype(jnp.float32) * (2.0 * math.pi / GRID)
    return (jnp.cos(angles), direction_sign * jnp.sin(angles))


def complex_product(formula, left_term, right_term):

    def complex_single(first, second):
        return jnp.einsum(formula, first, second, precision=EXACT_PRECISION)

    real_part = complex_single(left_term[0], right_term[0]) - complex_single(
        left_term[1], right_term[1]
    )
    imag_part = complex_single(left_term[0], right_term[1]) + complex_single(
        left_term[1], right_term[0]
    )
    return (real_part, imag_part)


def pointwise_product(left_term, right_term):
    real_part = left_term[0] * right_term[0] - left_term[1] * right_term[1]
    imag_part = left_term[0] * right_term[1] + left_term[1] * right_term[0]
    return (real_part, imag_part)


def forward_last(halves):
    in_shape = halves[0].shape
    outer_len = GRID // RADIX
    reshaped = tuple((member.reshape(in_shape[:-1] + (outer_len, RADIX)) for member in halves))
    section = complex_product("ka,...ab->...kb", tables(outer_len, -1.0), reshaped)
    section = pointwise_product(section, twiddle(outer_len, -1.0))
    section = complex_product("...kb,bq->...kq", section, tables(RADIX, -1.0))
    return tuple((member.reshape(in_shape) for member in section))


def inverse_last(halves):
    in_shape = halves[0].shape
    outer_len = GRID // RADIX
    reshaped = tuple((member.reshape(in_shape[:-1] + (outer_len, RADIX)) for member in halves))
    section = complex_product("...kq,qb->...kb", reshaped, tables(RADIX, 1.0))
    section = pointwise_product(section, twiddle(outer_len, 1.0))
    section = complex_product("ak,...kb->...ab", tables(outer_len, 1.0), section)
    return tuple((member.reshape(in_shape) / GRID for member in section))


def forward_rows(halves):
    in_shape = halves[0].shape
    outer_len = GRID // RADIX
    reshaped = tuple(
        (member.reshape(in_shape[:-2] + (outer_len, RADIX, in_shape[-1])) for member in halves)
    )
    section = complex_product("ka,...abc->...kbc", tables(outer_len, -1.0), reshaped)
    section = pointwise_product(
        section, tuple((member[:, :, None] for member in twiddle(outer_len, -1.0)))
    )
    section = complex_product("...kbc,bq->...kqc", section, tables(RADIX, -1.0))
    return tuple((member.reshape(in_shape) for member in section))


def inverse_rows(halves):
    in_shape = halves[0].shape
    outer_len = GRID // RADIX
    reshaped = tuple(
        (member.reshape(in_shape[:-2] + (outer_len, RADIX, in_shape[-1])) for member in halves)
    )
    section = complex_product("...kqc,qb->...kbc", reshaped, tables(RADIX, 1.0))
    section = pointwise_product(
        section, tuple((member[:, :, None] for member in twiddle(outer_len, 1.0)))
    )
    section = complex_product("ak,...kbc->...abc", tables(outer_len, 1.0), section)
    return tuple((member.reshape(in_shape) / GRID for member in section))


def permuted_frequency(indices):
    outer_len = GRID // RADIX
    natural = indices // RADIX + outer_len * (indices % RADIX)
    return jnp.where(natural < GRID // 2, natural, natural - GRID)


def propagator_block(first_column, column_count):
    row_freq = permuted_frequency(jnp.arange(GRID, dtype=jnp.int32))
    col_freq = permuted_frequency(first_column + jnp.arange(column_count, dtype=jnp.int32))
    radius = row_freq[:, None] * row_freq[:, None] + col_freq[None, :] * col_freq[None, :]
    phase_angle = radius.astype(jnp.float32) * (math.pi * FRESNEL / GRID)
    inside = 9 * radius <= GRID * GRID
    return (
        jnp.where(inside, jnp.cos(phase_angle), 0.0),
        jnp.where(inside, -jnp.sin(phase_angle), 0.0),
    )


def coefficients(positions, wave_index, wave_weight, wave_phase):
    grid_rows = positions[:, 0:1]
    grid_cols = positions[:, 1:2]
    turns = (
        FACTOR * (grid_rows * wave_index[None, :, 0] + grid_cols * wave_index[None, :, 1]) % GRID
    )
    angles = wave_phase[None, :] - turns.astype(jnp.float32) * (2.0 * math.pi / GRID)
    return (wave_weight[None, :] * jnp.cos(angles), wave_weight[None, :] * jnp.sin(angles))


def wrap_columns(stacked):
    return jnp.concatenate((stacked[..., GRID - HALF :], stacked, stacked[..., :HALF]), axis=-1)


def windows(extended, row_starts, col_starts, weights):
    wave_count = extended.shape[1]

    def windows_single(row_start, col_start, weight_re, weight_im):
        zero_index = jnp.zeros((), jnp.int32)
        window_cut = lax.dynamic_slice(
            extended,
            (zero_index, zero_index, row_start, col_start),
            (2, wave_count, WINDOW, WINDOW),
        )
        real_part = jnp.einsum(
            "w,wij->ij", weight_re, window_cut[0], precision=EXACT_PRECISION
        ) - jnp.einsum("w,wij->ij", weight_im, window_cut[1], precision=EXACT_PRECISION)
        imag_part = jnp.einsum(
            "w,wij->ij", weight_re, window_cut[1], precision=EXACT_PRECISION
        ) + jnp.einsum("w,wij->ij", weight_im, window_cut[0], precision=EXACT_PRECISION)
        return jnp.stack((real_part, imag_part))

    return jax.vmap(windows_single)(row_starts, col_starts, weights[0], weights[1])


def along_cols(halves, dft_table):
    return complex_product("...ij,jk->...ik", halves, dft_table)


def along_rows(halves, dft_table):
    return complex_product("ki,...ij->...kj", dft_table, halves)


def shards(plane_waves, transmission, wave_index, wave_weight, wave_phase, probe_pos):
    rows_here = plane_waves.shape[2]
    row_rank = lax.axis_index("row")
    row_count = lax.axis_size("row")
    propagator_values = propagator_block(row_rank * rows_here, rows_here)
    fields = (plane_waves[0], plane_waves[1])
    fields = pointwise_product(fields, (transmission[0, 0], transmission[0, 1]))
    fields = forward_last(fields)
    column_block = lax.all_to_all(jnp.stack(fields), "row", split_axis=3, concat_axis=2, tiled=True)
    halves = forward_rows((column_block[0], column_block[1]))
    halves = pointwise_product(halves, propagator_values)
    halves = inverse_rows(halves)
    exchanged = lax.all_to_all(jnp.stack(halves), "row", split_axis=2, concat_axis=3, tiled=True)
    fields = inverse_last((exchanged[0], exchanged[1]))
    stacked = jnp.stack(fields)
    probe_count = probe_pos.shape[0] // row_count
    extended = padded(stacked, (("row", 2),), HALF)
    extended = wrap_columns(extended)
    own_probes = lax.dynamic_slice_in_dim(probe_pos, row_rank * probe_count, probe_count, 0)
    row_starts = own_probes[:, 0] - row_rank * rows_here
    weights = coefficients(own_probes, wave_index, wave_weight, wave_phase)
    partial_value = windows(extended, row_starts, own_probes[:, 1], weights)
    dft_table = tables(WINDOW, -1.0)
    halves = (partial_value[:, 0], partial_value[:, 1])
    wave_count = lax.axis_size("wave")
    half_done = along_rows(halves, dft_table)
    summed = lax.psum_scatter(jnp.stack(half_done, axis=1), "wave", scatter_dimension=2, tiled=True)
    summed = jnp.stack(along_cols((summed[:, 0], summed[:, 1]), dft_table), axis=1)
    total_waves = plane_waves.shape[1] * wave_count
    return (summed[:, 0] * summed[:, 0] + summed[:, 1] * summed[:, 1]) / (
        WINDOW * WINDOW * total_waves
    )


def solution(mesh):
    return jax.shard_map(
        shards,
        mesh=mesh,
        in_specs=(
            P(None, "wave", "row", None),
            P(None, None, "row", None),
            P("wave", None),
            P("wave"),
            P("wave"),
            P(),
        ),
        out_specs=P("row", "wave", None),
        check_vma=False,
    )
```

profile of v0, /device:TPU:0, one launch (start us, length us, event | category | flops | bytes accessed | tf_op | source)
XLA Modules:
  0.0 549.7 jit_solution(2807459312730513669)
XLA Ops:
  6.5 3.9 fusion.454
  13.4 4.8 fusion.453
  25.8 4.0 multiply_subtract_fusion.1
  29.8 4.6 fusion.67
  34.4 4.6 fusion.65
  39.3 5.0 fusion.73
  44.3 4.6 fusion.30
  48.9 3.3 fusion.59
  52.3 3.3 fusion.57
  55.6 3.6 fusion.79
  59.2 8.6 %copy.196 = f32[1,1,256,2048]{2,0,1,3:T(1,128)S(1)} copy(f32[1,1,256,2048]{2,3,1,0:T(8,128)S(1)} %bitcast.331) | data formatting | bytes 4194304 | tf_op jit(solution)/shard_map/stack;reshape | solution.py:182
  67.8 3.4 fusion.82
  71.1 8.6 %copy.197 = f32[1,1,256,2048]{2,0,1,3:T(1,128)S(1)} copy(f32[1,1,256,2048]{2,3,1,0:T(8,128)S(1)} %bitcast.330) | data formatting | bytes 4194304 | tf_op jit(solution)/shard_map/stack;reshape | solution.py:182
  79.7 5.0 pad_maximum_fusion.6
  84.7 6.3 %all-to-all-start = ((f32[2,1,256,2048]{2,0,1,3:T(2,128)}), f32[2,1,256,2048]{2,0,1,3:T(2,128)}, u32[]{:S(2)}, u32[]{:S(2)}) async-start(f32[2,1,256,2048]{2,0,1,3:T(2,128)} %pad_maximum_fusion.6), calls=%async_computation | async-start | bytes 8388608 | tf_op jit(solution)/shard_map/all_to_all | solution.py:182
  91.1 94.0 %all-to-all-done = f32[2,1,256,2048]{2,0,1,3:T(2,128)} async-done(((f32[2,1,256,2048]{2,0,1,3:T(2,128)}), f32[2,1,256,2048]{2,0,1,3:T(2,128)}, u32[]{:S(2)}, u32[]{:S(2)}) %all-to-all-start) | async-done | bytes 4194336 | tf_op jit(solution)/shard_map/all_to_all | solution.py:182
  191.9 4.6 fusion.51
  196.5 4.6 fusion.49
  203.5 5.0 fusion.85
  208.5 4.2 fusion.26
  212.7 3.1 fusion.43
  215.8 3.3 fusion.41
  219.1 3.2 fusion.91
  222.3 3.1 fusion.94
  225.4 10.1 %fusion.139 = f32[64,32,256]{2,0,1:T(8,128)S(1)} fusion(f32[64,32,256]{2,0,1:T(8,128)S(1)} %fusion.94, f32[64,32,256]{2,0,1:T(8,128)S(1)} %fusion.91, s32[256]{0:T(256)S(1)} %fusion.268, s32[32,64]{1,0:T(8,128)S(1)} %fusion.186), kind=kOutput, calls=%fused_computation.177 | convolution fusion | flops 408477696 | bytes 6300672 | tf_op jit(solution)/shard_map/...kqc,qb->...kbc/dot_general | solution.py:48
  235.5 10.3 %fusion.150 = f32[64,32,256]{2,0,1:T(8,128)S(1)} fusion(f32[64,32,256]{2,0,1:T(8,128)S(1)} %fusion.94, f32[64,32,256]{2,0,1:T(8,128)S(1)} %fusion.91, s32[256]{0:T(256)S(1)} %fusion.268, s32[32,64]{1,0:T(8,128)S(1)} %fusion.186), kind=kOutput, calls=%fused_computation.188 | convolution fusion | flops 408477696 | bytes 6300672 | tf_op jit(solution)/shard_map/...kqc,qb->...kbc/dot_general | solution.py:48
  245.9 10.1 %fusion.152 = f32[64,32,256]{2,0,1:T(8,128)S(1)} fusion(f32[64,32,256]{2,0,1:T(8,128)S(1)} %fusion.94, f32[64,32,256]{2,0,1:T(8,128)S(1)} %fusion.91, s32[256]{0:T(256)S(1)} %fusion.268, s32[32,64]{1,0:T(8,128)S(1)} %fusion.186), kind=kOutput, calls=%fused_computation.190 | convolution fusion | flops 408477696 | bytes 6300672 | tf_op jit(solution)/shard_map/...kqc,qb->...kbc/dot_general | solution.py:48
  256.0 10.2 %fusion.141 = f32[64,32,256]{2,0,1:T(8,128)S(1)} fusion(f32[64,32,256]{2,0,1:T(8,128)S(1)} %fusion.94, f32[64,32,256]{2,0,1:T(8,128)S(1)} %fusion.91, s32[256]{0:T(256)S(1)} %fusion.268, s32[32,64]{1,0:T(8,128)S(1)} %fusion.186), kind=kOutput, calls=%fused_computation.179 | convolution fusion | flops 408477696 | bytes 6300672 | tf_op jit(solution)/shard_map/...kqc,qb->...kbc/dot_general | solution.py:48
  266.1 4.7 fusion.24
  282.2 11.7 %copy.218 = f32[2,1,2048,256]{3,1,0,2:T(1,128)} copy(f32[2,1,2048,256]{3,2,1,0:T(8,128)S(1)} %pad_maximum_fusion.7) | data formatting | bytes 8388608 | tf_op jit(solution)/shard_map/stack | solution.py:186
  293.9 4.6 all-to-all-start.1
  298.5 93.9 %all-to-all-done.1 = f32[2,1,2048,256]{3,1,0,2:T(1,128)} async-done(((f32[2,1,2048,256]{3,1,0,2:T(1,128)}), f32[2,1,2048,256]{3,1,0,2:T(1,128)}, u32[]{:S(2)}, u32[]{:S(2)}) %all-to-all-start.1) | async-done | bytes 4194336 | tf_op jit(solution)/shard_map/all_to_all | solution.py:186
  399.3 3.3 fusion.148
  402.7 3.5 fusion.136
  408.3 3.9 convolution_subtract_fusion
  412.2 3.1 multiply_subtract_fusion
  415.3 3.2 fusion.33
  418.6 3.2 fusion.35
  421.8 3.6 multiply_bitcast_fusion
  426.6 3.3 multiply_bitcast_fusion.1
  436.1 3.1 copy.229
  439.3 3.5 collective-permute-start.1
  446.2 14.3 %collective-permute-done = f32[2,1,64,2048]{3,2,1,0:T(8,128)} collective-permute-done((f32[2,1,64,2048]{3,2,1,0:T(8,128)S(1)}, f32[2,1,64,2048]{3,2,1,0:T(8,128)}, u32[]{:S(2)}, u32[]{:S(2)}) %collective-permute-start) | collective-permute-done | bytes 1048608 | tf_op jit(solution)/shard_map/ppermute | solution.py:22
  460.5 3.1 copy.230
  463.6 3.3 copy.231
  466.9 14.8 %fusion = f32[2,1,384,2176]{2,3,1,0:T(8,128)} fusion(f32[2,1,64,2048]{2,3,1,0:T(8,128)} %copy.231, f32[2,1,64,2048]{2,3,1,0:T(8,128)} %copy.230, f32[1,1,256,2048]{2,3,1,0:T(8,128)S(1)} %bitcast.318, f32[1,1,256,2048]{2,3,1,0:T(8,128)} %bitcast.320), kind=kLoop, calls=%fused_computation.4 | loop fusion | flops 18382848 | bytes 12976128 | tf_op jit(solution)/shard_map/concatenate | solution.py:142
  481.7 25.6 %while.1 = (s32[]{:T(128)}, f32[2,1,384,2176]{2,3,1,0:T(8,128)}, s32[8,4]{0,1:T(4,128)S(1)}, f32[8,2,1,128,128]{3,4,0,2,1:T(8,128)S(1)}, s32[]{:T(128)}) while((s32[]{:T(128)}, f32[2,1,384,2176]{2,3,1,0:T(8,128)}, s32[8,4]{0,1:T(4,128)S(1)}, f32[8,2,1,128,128]{3,4,0,2,1:T(8,128)S(1)}, s32[]{:T(128)}) %tuple.44), condition=%wide.while_cond, body=%wide.while_body.sunk | while | flops 2 | bytes 1048701 | solution.py:150
  512.4 26.3 %reduce-scatter.2.cloned.1.call-done = f32[8,2,32,128]{3,0,1,2:T(8,128)} async-done(((f32[8,2,128,128]{3,0,1,2:T(8,128)}), f32[8,2,32,128]{3,0,1,2:T(8,128)}) %reduce-scatter.2.cloned.1.call-update) | async-done | bytes 262160 | tf_op jit(solution)/shard_map/reduce_scatter | solution.py:200
  (118 shorter events, 83.8 us)
Async XLA Ops:
  6.5 436.3 %copy-start = (s32[64,2]{0,1:T(2,128)S(1)}, s32[64,2]{0,1:T(2,128)}, u32[]{:S(2)}) copy-start(s32[64,2]{0,1:T(2,128)} %param.11) | copy-start | bytes 1540
  39.3 5.0 copy-start.2
  84.7 100.4 %all-to-all-start = ((f32[2,1,256,2048]{2,0,1,3:T(2,128)}), f32[2,1,256,2048]{2,0,1,3:T(2,128)}, u32[]{:S(2)}, u32[]{:S(2)}) async-start(f32[2,1,256,2048]{2,0,1,3:T(2,128)} %pad_maximum_fusion.6), calls=%async_computation | async-start | bytes 8388608 | tf_op jit(solution)/shard_map/all_to_all | solution.py:182
  203.5 5.0 copy-start.4
  293.9 98.5 %all-to-all-start.1 = ((f32[2,1,2048,256]{3,1,0,2:T(1,128)}), f32[2,1,2048,256]{3,1,0,2:T(1,128)}, u32[]{:S(2)}, u32[]{:S(2)}) async-start(f32[2,1,2048,256]{3,1,0,2:T(1,128)} %copy.218), calls=%async_computation.1 | async-start | bytes 8388608 | tf_op jit(solution)/shard_map/all_to_all | solution.py:186
  298.5 240.3 %reduce-scatter.2.cloned.1.call-start = ((), (), s32[]{:S(2)}) async-start(), calls=%async_computation.3 | async-start | bytes 1310720 | tf_op jit(solution)/shard_map/reduce_scatter | solution.py:200
  408.3 3.9 copy-start.3
  431.2 2.7 copy-start.1
  436.0 8.1 %copy-start.6 = (s32[1,2]{1,0:T(1,128)S(1)}, s32[1,2]{1,0:T(1,128)}, u32[]{:S(2)}) copy-start(s32[1,2]{1,0:T(1,128)} %param.8) | copy-start | bytes 28
  436.1 24.4 %collective-permute-start = (f32[2,1,64,2048]{3,2,1,0:T(8,128)S(1)}, f32[2,1,64,2048]{3,2,1,0:T(8,128)}, u32[]{:S(2)}, u32[]{:S(2)}) collective-permute-start(f32[2,1,64,2048]{3,2,1,0:T(8,128)S(1)} %copy.228), channel_id=1, source_target_pairs={{0,1},{1,2},{2,3},{3,4},{4,5},{5,6},{6,7},{7,0},{8,9},{9,10},{10,1... | collective-permute-start | bytes 3145736 | tf_op jit(solution)/shard_map/ppermute | solution.py:22
  439.3 24.4 %collective-permute-start.1 = (f32[2,1,64,2048]{3,2,1,0:T(8,128)}, f32[2,1,64,2048]{3,2,1,0:T(8,128)}, u32[]{:S(2)}, u32[]{:S(2)}) collective-permute-start(f32[2,1,64,2048]{3,2,1,0:T(8,128)} %copy.229), channel_id=1, source_target_pairs={{1,0},{2,1},{3,2},{4,3},{5,4},{6,5},{7,6},{0,7},{9,8},{10,9},{11,1... | collective-permute-start | bytes 3145736 | tf_op jit(solution)/shard_map/ppermute | solution.py:25
  466.9 14.8 %copy-start.5 = (f32[8,2,1,128,128]{3,4,0,2,1:T(8,128)S(1)}, f32[8,2,1,128,128]{3,4,0,2,1:T(8,128)}, u32[]{:S(2)}) copy-start(f32[8,2,1,128,128]{3,4,0,2,1:T(8,128)} %custom-call) | copy-start | bytes 3145732
Sparse Core Ops, SparseCore 0:
  512.6 26.1 reduce-scatter.1
where the time goes:
time: 561 us; the launch traced here: 550 us
  waiting for transfers between devices  229 us (41%)
  matrix products  145 us (26%)
  local copies, waits for them, and re-layouts  112 us (20%)
  other arithmetic  33.4 us (6%)
  between operations  15.7 us (3%)
  starting transfers between devices  14.5 us (3%)
    dot_general x40, matrix products, complex_single(): return jnp.einsum(formula, first, second, precision=EXACT_PRECISION)  145 us
    all_to_all x1, waiting for transfers between devices, shards(): lax.all_to_all(jnp.stack(fields), 'row', split_axis=3, concat_axis=2, til...  94 us
    all_to_all x1, waiting for transfers between devices, shards(): lax.all_to_all(jnp.stack(halves), 'row', split_axis=2, concat_axis=3, til...  93.9 us
    reduce_scatter x1, waiting for transfers between devices, shards(): lax.psum_scatter(jnp.stack(half_done, axis=1), 'wave', scatter_dimension=...  26.3 us
    gather x48, local copies, waits for them, and re-layouts  25.3 us
    another operation x2, local copies, waits for them, and re-layouts, shards(): jnp.stack(fields)  17.1 us
    concatenate x1, other arithmetic, wrap_columns(): jnp.concatenate((stacked[..., GRID - HALF:], stacked, stacked[..., :HALF]...  14.8 us
    ppermute x1, waiting for transfers between devices, padded(): lax.ppermute(lax.slice_in_dim(block, block.shape[dim] - width, None, axis...  14.3 us
  transfers between devices with their start and end apart: 5, of which 4 were waited for; matrix products, arithmetic and copies ran while one was open for 2% of the time, Pallas kernels for 0%

commit v1 on v0

--- a/solution.py
+++ b/solution.py
@@ -179,7 +179,11 @@
     fields = (plane_waves[0], plane_waves[1])
     fields = pointwise_product(fields, (transmission[0, 0], transmission[0, 1]))
     fields = forward_last(fields)
-    column_block = lax.all_to_all(jnp.stack(fields), "row", split_axis=3, concat_axis=2, tiled=True)
+    part = jnp.stack(fields)
+    size = lax.axis_size("row")
+    blocks = jnp.stack(jnp.split(part, size, axis=3), axis=0)
+    blocks = lax.all_to_all(blocks, "row", split_axis=0, concat_axis=0)
+    column_block = jnp.concatenate(blocks, axis=2)
     halves = forward_rows((column_block[0], column_block[1]))
     halves = pointwise_product(halves, propagator_values)
     halves = inverse_rows(halves)

time: 561 us -> 561 us (level)
  local copies, waits for them, and re-layouts: 112 us -> 94 us
  matrix products: 145 us -> 159 us
    dot_general x40, matrix products: 145 us -> 159 us  [complex_single(): return jnp.einsum(formula, first, second, precision=EXACT_PRECISION)]
    another operation x3, local copies, waits for them, and re-layouts: 17.1 us -> 4.85 us  [the longest x2 4.85 us: shards(): part = jnp.stack(fields)]
    unnamed x1 -> x8, other arithmetic: 0.01 us -> 7.09 us
    slice x3 -> x1, local copies, waits for them, and re-layouts: 6.64 us -> 0.39 us  [shards(): halves = forward_rows((column_block[0], column_block[1]))]
where the time goes in v1:
time: 561 us; the launch traced here: 550 us
  waiting for transfers between devices  230 us (41%)
  matrix products  159 us (28%)
  local copies, waits for them, and re-layouts  94 us (17%)
  other arithmetic  36.6 us (7%)
  between operations  15.6 us (3%)
  starting transfers between devices  14.5 us (3%)
    dot_general x40, matrix products, complex_single(): return jnp.einsum(formula, first, second, precision=EXACT_PRECISION)  159 us
    all_to_all x1, waiting for transfers between devices, shards(): blocks = lax.all_to_all(blocks, 'row', split_axis=0, concat_axis=0)  94 us
    all_to_all x1, waiting for transfers between devices, shards(): lax.all_to_all(jnp.stack(halves), 'row', split_axis=2, concat_axis=3, til...  93.9 us
    reduce_scatter x1, waiting for transfers between devices, shards(): lax.psum_scatter(jnp.stack(half_done, axis=1), 'wave', scatter_dimension=...  28.3 us
    gather x48, local copies, waits for them, and re-layouts  25.7 us
    concatenate x1, other arithmetic, wrap_columns(): jnp.concatenate((stacked[..., GRID - HALF:], stacked, stacked[..., :HALF]...  14.8 us
    ppermute x1, waiting for transfers between devices, padded(): lax.ppermute(lax.slice_in_dim(block, block.shape[dim] - width, None, axis...  14.1 us
    another operation x1, local copies, waits for them, and re-layouts, shards(): jnp.stack(halves)  12.1 us
  transfers between devices with their start and end apart: 5, of which 4 were waited for; matrix products, arithmetic and copies ran while one was open for 2% of the time, Pallas kernels for 0%

profile of v1, /device:TPU:0, one launch (start us, length us, event | category | flops | bytes accessed | tf_op | source)
XLA Modules:
  0.0 550.1 jit_solution(14686526953074682180)
XLA Ops:
  6.5 3.9 fusion.477
  10.5 2.9 copy.219
  13.4 4.8 fusion.476
  22.9 2.9 copy.222
  25.8 4.0 multiply_subtract_fusion.1
  29.9 4.6 fusion.67
  34.5 4.6 fusion.65
  39.4 5.0 fusion.73
  44.4 4.5 fusion.30
  48.9 3.3 fusion.57
  52.2 4.6 fusion.59
  56.9 16.4 %fusion.82 = f32[256,32,64]{0,2,1:T(8,128)} fusion(f32[256,32,64]{0,2,1:T(8,128)S(1)} %fusion.57, f32[256,32,64]{0,1,2:T(8,128)S(1)} %get-tuple-element.43), kind=kOutput, calls=%fused_computation.128 | convolution fusion | flops 403238912 | bytes 6291456 | tf_op jit(solution)/shard_map/...kb,bq->...kq/dot_general | solution.py:48
  75.2 6.8 %fusion.79 = f32[256,32,64]{0,2,1:T(8,128)} fusion(f32[256,32,64]{0,2,1:T(8,128)} %fusion.59, f32[256,32,64]{0,1,2:T(8,128)} %copy-done.2), kind=kOutput, calls=%fused_computation.127 | convolution fusion | flops 403234816 | bytes 6291456 | tf_op jit(solution)/shard_map/...kb,bq->...kq/dot_general | solution.py:48
  82.0 2.9 copy.169
  92.9 6.4 %all-to-all-start = ((f32[8,2,1,256,256]{4,3,2,1,0:T(8,128)}), f32[8,2,1,256,256]{4,3,2,1,0:T(8,128)}, u32[]{:S(2)}, u32[]{:S(2)}) async-start(f32[8,2,1,256,256]{4,3,2,1,0:T(8,128)} %fusion.133), calls=%async_computation | async-start | bytes 8388608 | tf_op jit(solution)/shard_map/all_to_all | solution.py:185
  99.4 94.0 %all-to-all-done = f32[8,2,1,256,256]{4,3,2,1,0:T(8,128)} async-done(((f32[8,2,1,256,256]{4,3,2,1,0:T(8,128)}), f32[8,2,1,256,256]{4,3,2,1,0:T(8,128)}, u32[]{:S(2)}, u32[]{:S(2)}) %all-to-all-start) | async-done | bytes 4194336 | tf_op jit(solution)/shard_map/all_to_all | solution.py:185
  196.3 3.3 fusion.51
  199.6 3.3 fusion.49
  202.9 3.3 fusion.85
  206.2 4.6 fusion.26
  210.8 3.1 fusion.43
  213.9 3.1 fusion.41
  217.0 3.1 fusion.91
  220.1 3.3 fusion.94
  223.5 10.2 %fusion.162 = f32[64,32,256]{2,0,1:T(8,128)S(1)} fusion(f32[64,32,256]{2,0,1:T(8,128)S(1)} %fusion.94, f32[64,32,256]{2,0,1:T(8,128)S(1)} %fusion.91, s32[256]{0:T(256)S(1)} %fusion.291, s32[32,64]{1,0:T(8,128)S(1)} %fusion.209), kind=kOutput, calls=%fused_computation.215 | convolution fusion | flops 408477696 | bytes 6300672 | tf_op jit(solution)/shard_map/...kqc,qb->...kbc/dot_general | solution.py:48
  233.6 9.9 %fusion.173 = f32[64,32,256]{2,0,1:T(8,128)S(1)} fusion(f32[64,32,256]{2,0,1:T(8,128)S(1)} %fusion.94, f32[64,32,256]{2,0,1:T(8,128)S(1)} %fusion.91, s32[256]{0:T(256)S(1)} %fusion.291, s32[32,64]{1,0:T(8,128)S(1)} %fusion.209), kind=kOutput, calls=%fused_computation.226 | convolution fusion | flops 408477696 | bytes 6300672 | tf_op jit(solution)/shard_map/...kqc,qb->...kbc/dot_general | solution.py:48
  243.6 10.3 %fusion.175 = f32[64,32,256]{2,0,1:T(8,128)S(1)} fusion(f32[64,32,256]{2,0,1:T(8,128)S(1)} %fusion.94, f32[64,32,256]{2,0,1:T(8,128)S(1)} %fusion.91, s32[256]{0:T(256)S(1)} %fusion.291, s32[32,64]{1,0:T(8,128)S(1)} %fusion.209), kind=kOutput, calls=%fused_computation.228 | convolution fusion | flops 408477696 | bytes 6300672 | tf_op jit(solution)/shard_map/...kqc,qb->...kbc/dot_general | solution.py:48
  253.9 10.1 %fusion.164 = f32[64,32,256]{2,0,1:T(8,128)S(1)} fusion(f32[64,32,256]{2,0,1:T(8,128)S(1)} %fusion.94, f32[64,32,256]{2,0,1:T(8,128)S(1)} %fusion.91, s32[256]{0:T(256)S(1)} %fusion.291, s32[32,64]{1,0:T(8,128)S(1)} %fusion.209), kind=kOutput, calls=%fused_computation.217 | convolution fusion | flops 408477696 | bytes 6300672 | tf_op jit(solution)/shard_map/...kqc,qb->...kbc/dot_general | solution.py:48
  264.0 5.0 fusion.24
  279.8 12.1 %copy.196 = f32[2,1,2048,256]{3,1,0,2:T(1,128)} copy(f32[2,1,2048,256]{3,2,1,0:T(8,128)S(1)} %pad_maximum_fusion.6) | data formatting | bytes 8388608 | tf_op jit(solution)/shard_map/stack | solution.py:190
  292.0 4.6 all-to-all-start.1
  296.6 93.9 %all-to-all-done.1 = f32[2,1,2048,256]{3,1,0,2:T(1,128)} async-done(((f32[2,1,2048,256]{3,1,0,2:T(1,128)}), f32[2,1,2048,256]{3,1,0,2:T(1,128)}, u32[]{:S(2)}, u32[]{:S(2)}) %all-to-all-start.1) | async-done | bytes 4194336 | tf_op jit(solution)/shard_map/all_to_all | solution.py:190
  397.4 3.4 fusion.171
  400.7 3.5 fusion.159
  406.3 3.9 convolution_subtract_fusion
  410.2 3.1 multiply_subtract_fusion
  413.4 3.2 fusion.33
  416.6 3.2 fusion.35
  419.9 3.6 multiply_bitcast_fusion
  424.7 3.3 multiply_bitcast_fusion.1
  434.2 3.1 copy.207
  437.3 3.5 collective-permute-start.1
  444.4 14.1 %collective-permute-done = f32[2,1,64,2048]{3,2,1,0:T(8,128)} collective-permute-done((f32[2,1,64,2048]{3,2,1,0:T(8,128)S(1)}, f32[2,1,64,2048]{3,2,1,0:T(8,128)}, u32[]{:S(2)}, u32[]{:S(2)}) %collective-permute-start) | collective-permute-done | bytes 1048608 | tf_op jit(solution)/shard_map/ppermute | solution.py:22
  458.5 3.2 copy.208
  461.6 3.3 copy.209
  464.9 14.8 %fusion = f32[2,1,384,2176]{2,3,1,0:T(8,128)} fusion(f32[2,1,64,2048]{2,3,1,0:T(8,128)} %copy.209, f32[2,1,64,2048]{2,3,1,0:T(8,128)} %copy.208, f32[1,1,256,2048]{2,3,1,0:T(8,128)S(1)} %bitcast.364, f32[1,1,256,2048]{2,3,1,0:T(8,128)} %bitcast.366), kind=kLoop, calls=%fused_computation.18 | loop fusion | flops 18382848 | bytes 12976128 | tf_op jit(solution)/shard_map/concatenate | solution.py:142
  479.7 26.1 %while.1 = (s32[]{:T(128)}, f32[2,1,384,2176]{2,3,1,0:T(8,128)}, s32[8,4]{0,1:T(4,128)S(1)}, f32[8,2,1,128,128]{3,4,0,2,1:T(8,128)S(1)}, s32[]{:T(128)}) while((s32[]{:T(128)}, f32[2,1,384,2176]{2,3,1,0:T(8,128)}, s32[8,4]{0,1:T(4,128)S(1)}, f32[8,2,1,128,128]{3,4,0,2,1:T(8,128)S(1)}, s32[]{:T(128)}) %tuple.43), condition=%wide.while_cond, body=%wide.while_body.sunk | while | flops 2 | bytes 1048701 | solution.py:150
  510.9 28.3 %reduce-scatter.2.cloned.1.call-done = f32[8,2,32,128]{3,0,1,2:T(8,128)} async-done(((f32[8,2,128,128]{3,0,1,2:T(8,128)}), f32[8,2,32,128]{3,0,1,2:T(8,128)}) %reduce-scatter.2.cloned.1.call-update) | async-done | bytes 262160 | tf_op jit(solution)/shard_map/reduce_scatter | solution.py:204
  (125 shorter events, 81.8 us)
Async XLA Ops:
  6.5 434.3 %copy-start = (s32[64,2]{0,1:T(2,128)S(1)}, s32[64,2]{0,1:T(2,128)}, u32[]{:S(2)}) copy-start(s32[64,2]{0,1:T(2,128)} %param.11) | copy-start | bytes 1540
  39.4 5.0 copy-start.4
  48.9 8.0 %copy-start.2 = (f32[256,32,64]{0,1,2:T(8,128)}, f32[256,32,64]{0,1,2:T(8,128)S(1)}, u32[]{:S(2)}) copy-start(f32[256,32,64]{0,1,2:T(8,128)S(1)} %get-tuple-element.43) | copy-start | bytes 6291460
  84.9 2.0 copy-start.1
  92.9 100.4 %all-to-all-start = ((f32[8,2,1,256,256]{4,3,2,1,0:T(8,128)}), f32[8,2,1,256,256]{4,3,2,1,0:T(8,128)}, u32[]{:S(2)}, u32[]{:S(2)}) async-start(f32[8,2,1,256,256]{4,3,2,1,0:T(8,128)} %fusion.133), calls=%async_computation | async-start | bytes 8388608 | tf_op jit(solution)/shard_map/all_to_all | solution.py:185
  292.0 98.5 %all-to-all-start.1 = ((f32[2,1,2048,256]{3,1,0,2:T(1,128)}), f32[2,1,2048,256]{3,1,0,2:T(1,128)}, u32[]{:S(2)}, u32[]{:S(2)}) async-start(f32[2,1,2048,256]{3,1,0,2:T(1,128)} %copy.196), calls=%async_computation.1 | async-start | bytes 8388608 | tf_op jit(solution)/shard_map/all_to_all | solution.py:190
  296.5 242.6 %reduce-scatter.2.cloned.1.call-start = ((), (), s32[]{:S(2)}) async-start(), calls=%async_computation.3 | async-start | bytes 1310720 | tf_op jit(solution)/shard_map/reduce_scatter | solution.py:204
  406.3 3.9 copy-start.5
  429.2 2.7 copy-start.3
  434.1 8.1 %copy-start.7 = (s32[1,2]{1,0:T(1,128)S(1)}, s32[1,2]{1,0:T(1,128)}, u32[]{:S(2)}) copy-start(s32[1,2]{1,0:T(1,128)} %param.8) | copy-start | bytes 28
  434.1 24.3 %collective-permute-start = (f32[2,1,64,2048]{3,2,1,0:T(8,128)S(1)}, f32[2,1,64,2048]{3,2,1,0:T(8,128)}, u32[]{:S(2)}, u32[]{:S(2)}) collective-permute-start(f32[2,1,64,2048]{3,2,1,0:T(8,128)S(1)} %copy.206), channel_id=1, source_target_pairs={{0,1},{1,2},{2,3},{3,4},{4,5},{5,6},{6,7},{7,0},{8,9},{9,10},{10,1... | collective-permute-start | bytes 3145736 | tf_op jit(solution)/shard_map/ppermute | solution.py:22
  437.3 24.3 %collective-permute-start.1 = (f32[2,1,64,2048]{3,2,1,0:T(8,128)}, f32[2,1,64,2048]{3,2,1,0:T(8,128)}, u32[]{:S(2)}, u32[]{:S(2)}) collective-permute-start(f32[2,1,64,2048]{3,2,1,0:T(8,128)} %copy.207), channel_id=1, source_target_pairs={{1,0},{2,1},{3,2},{4,3},{5,4},{6,5},{7,6},{0,7},{9,8},{10,9},{11,1... | collective-permute-start | bytes 3145736 | tf_op jit(solution)/shard_map/ppermute | solution.py:25
  464.9 14.8 %copy-start.6 = (f32[8,2,1,128,128]{3,4,0,2,1:T(8,128)S(1)}, f32[8,2,1,128,128]{3,4,0,2,1:T(8,128)}, u32[]{:S(2)}) copy-start(f32[8,2,1,128,128]{3,4,0,2,1:T(8,128)} %custom-call.1) | copy-start | bytes 3145732
Sparse Core Ops, SparseCore 0:
  511.0 28.1 reduce-scatter.1
